TPU v7x, 512 devices: a whole 4x8x8 slice. The times are simulated.
512 devices in a mesh: crate: 32 (over z, x), board: 16 (over y, core).
Axes of the slice: x: 4, y: 8, z: 8, core: 2. Of those that a mesh axis runs over, the one named last changes fastest.
Arguments:
- voltages: bfloat16 [2048, 65536], P(('crate', 'board')), may hold values from -6 to 6
- wiring: int32 [2048], replicated, may hold values from 0 to 2047, each once
- positions: float32 [2, 2048], replicated, may hold values from -4 to 4
- directions: float32 [2, 512], replicated, may hold values from -1 to 1
- gains: float32 [2, 256, 2048], P(None, 'crate'), may hold values from -6 to 6
- delays: int32 [256, 512], replicated, may hold values from 0 to 31
Outputs:
- dedispersed: float32 [512, 512, 32], P('crate', 'board')
Inputs may be any that keep to these rules, and one draw needn't show every extreme that they name: `wiring`: each of the 2048 antennas is wired to exactly one input row.
All inputs are finite; a program needn't handle non-finite values.
Results may differ from a plain program's by a relative error of at most 0.0096.
Values may be sent and summed in bfloat16 or wider, within the bound.
A program may use at most 64 MiB of HBM per device.

v0:
```python
import math
import jax
import jax.numpy as jnp
from jax import lax
from jax.sharding import PartitionSpec as P

ANTENNA_INPUTS = 2048
FREQ_CHANNELS = 256
FRAME_SAMPLES = 512
BEAMS = 512
DMS = 512
SPECTRUM_BATCHES = 2
BATCH_SPECTRA = 64
AVG = 4
BINS = 16
TB = 32
two_pi = 2.0 * math.pi


def filter_table():
    sample_ids = jnp.arange(FRAME_SAMPLES, dtype=jnp.int32)
    column_ids = jnp.arange(FREQ_CHANNELS, dtype=jnp.int32)
    window = 0.5 - 0.5 * jnp.cos(two_pi / FRAME_SAMPLES * sample_ids.astype(jnp.float32))
    turn_ids = sample_ids[:, None] * column_ids[None, :] % FRAME_SAMPLES
    phase_angle = two_pi / FRAME_SAMPLES * turn_ids.astype(jnp.float32)
    scale_norm_factor = 1.0 / math.sqrt(3.0 * FRAME_SAMPLES / 8.0)
    real_part = window[:, None] * jnp.cos(phase_angle) * scale_norm_factor
    imag_part = -window[:, None] * jnp.sin(phase_angle) * scale_norm_factor
    return jnp.concatenate([real_part, imag_part], axis=1).astype(jnp.bfloat16)


def beam_weights(channel, directions, place_x, place_y, gain_re, gain_im):
    geo_delay = (
        directions[0][:, None] * place_x[None, :] + directions[1][:, None] * place_y[None, :]
    )
    factor = two_pi * (1.0 + channel.astype(jnp.float32) / FREQ_CHANNELS)
    phase_angle = factor * geo_delay
    cosine = jnp.cos(phase_angle)
    sine_value = jnp.sin(phase_angle)
    scale_norm_factor = 1.0 / math.sqrt(ANTENNA_INPUTS)
    weight_re = (
        (gain_re[None, :] * cosine + gain_im[None, :] * sine_value) * scale_norm_factor
    ).astype(jnp.bfloat16)
    weight_im = (
        (gain_im[None, :] * cosine - gain_re[None, :] * sine_value) * scale_norm_factor
    ).astype(jnp.bfloat16)
    return (weight_re, weight_im)


def dedisperse(series, delay_table):
    bin_count = series.shape[2]
    bin_ids = jnp.arange(bin_count, dtype=jnp.int32)
    turn_ids = bin_ids[:, None] * bin_ids[None, :] % bin_count
    phase_angle = two_pi / bin_count * turn_ids.astype(jnp.float32)
    cos_table = jnp.cos(phase_angle)
    sin_table = jnp.sin(phase_angle)
    spec_re = jnp.einsum("bct,tk->kcb", series, cos_table, precision=lax.Precision.HIGHEST)
    spec_im = -jnp.einsum("bct,tk->kcb", series, sin_table, precision=lax.Precision.HIGHEST)

    def per_freq(inputs):
        freq_id, part_re, part_im = inputs
        shift_angle = two_pi / bin_count * (freq_id * delay_table % bin_count).astype(jnp.float32)
        shift_re = jnp.cos(shift_angle)
        shift_im = jnp.sin(shift_angle)
        out_re = jnp.einsum(
            "cd,cb->db", shift_re, part_re, precision=lax.Precision.HIGHEST
        ) - jnp.einsum("cd,cb->db", shift_im, part_im, precision=lax.Precision.HIGHEST)
        out_im = jnp.einsum(
            "cd,cb->db", shift_re, part_im, precision=lax.Precision.HIGHEST
        ) + jnp.einsum("cd,cb->db", shift_im, part_re, precision=lax.Precision.HIGHEST)
        return (out_re, out_im)

    freq_re, freq_im = lax.map(per_freq, (bin_ids, spec_re, spec_im))
    keep_mask = (bin_ids > 0).astype(jnp.float32)[:, None]
    scale_norm_factor = 1.0 / (bin_count * math.sqrt(FREQ_CHANNELS))
    first_term = jnp.einsum(
        "kdb,kt->bdt", freq_re, cos_table * keep_mask, precision=lax.Precision.HIGHEST
    )
    second_term = jnp.einsum(
        "kdb,kt->bdt", freq_im, sin_table * keep_mask, precision=lax.Precision.HIGHEST
    )
    return (first_term - second_term) * scale_norm_factor


def shards(voltages, wiring, positions, directions, gains, delays):
    crate_list = lax.axis_size("crate")
    board_list = lax.axis_size("board")
    crate_index = lax.axis_index("crate")
    board_index = lax.axis_index("board")
    local_antenna = voltages.shape[0]
    channel_groups = SPECTRUM_BATCHES * FREQ_CHANNELS // (crate_list * board_list)
    dft_table = filter_table()
    sample_frames = voltages.reshape(
        local_antenna * SPECTRUM_BATCHES * BATCH_SPECTRA, FRAME_SAMPLES
    )
    spectrum_rows = jnp.dot(sample_frames, dft_table, preferred_element_type=jnp.float32).astype(
        jnp.bfloat16
    )
    spectrum_rows = spectrum_rows.reshape(
        local_antenna, SPECTRUM_BATCHES, BATCH_SPECTRA, 2, FREQ_CHANNELS
    ).transpose(4, 1, 0, 3, 2)
    spectrum_rows = spectrum_rows.reshape(
        crate_list, board_list, channel_groups, local_antenna, 2 * BATCH_SPECTRA
    )
    position_grid = jnp.arange(ANTENNA_INPUTS, dtype=jnp.int32).reshape(
        crate_list, board_list, local_antenna
    )
    received_data = lax.all_to_all(
        lax.all_to_all(spectrum_rows, "crate", split_axis=0, concat_axis=3, tiled=True),
        "board",
        split_axis=1,
        concat_axis=3,
        tiled=True,
    )
    position_ids = position_grid.transpose(1, 0, 2).reshape(ANTENNA_INPUTS)
    received_data = received_data.reshape(channel_groups, ANTENNA_INPUTS, 2 * BATCH_SPECTRA)
    antenna = jnp.take(wiring, position_ids)
    place_x = jnp.take(positions[0], antenna)
    place_y = jnp.take(positions[1], antenna)
    gains_slot = jnp.take(gains, antenna, axis=2)
    gain_rows = gains.shape[1]
    first_group = (crate_index * board_list + board_index) * channel_groups
    beam_block = 256
    block_count = BEAMS // beam_block
    dir_blocks = directions.reshape(2, block_count, beam_block).transpose(1, 0, 2)

    def group_power(inputs):
        group_id, columns = inputs
        whole_id = first_group + group_id
        channel = whole_id // SPECTRUM_BATCHES
        gain_row = channel - crate_index * gain_rows
        gain_re = lax.dynamic_index_in_dim(gains_slot[0], gain_row, 0, keepdims=False)
        gain_im = lax.dynamic_index_in_dim(gains_slot[1], gain_row, 0, keepdims=False)

        def block_power(dir_block):
            weight_re, weight_im = beam_weights(
                channel, dir_block, place_x, place_y, gain_re, gain_im
            )
            real_side = jnp.dot(weight_re, columns, preferred_element_type=jnp.float32)
            imag_side = jnp.dot(weight_im, columns, preferred_element_type=jnp.float32)
            beam_re = real_side[:, :BATCH_SPECTRA] - imag_side[:, BATCH_SPECTRA:]
            beam_im = real_side[:, BATCH_SPECTRA:] + imag_side[:, :BATCH_SPECTRA]
            beam_power = (
                (beam_re * beam_re + beam_im * beam_im).reshape(beam_block, BINS, AVG).mean(axis=2)
            )
            return beam_power.astype(jnp.bfloat16)

        return lax.map(block_power, dir_blocks).reshape(BEAMS, BINS)

    powers = lax.map(group_power, (jnp.arange(channel_groups, dtype=jnp.int32), received_data))
    beam_local = BEAMS // crate_list
    dm_local = DMS // board_list
    dm_delays = lax.dynamic_slice_in_dim(delays, board_index * dm_local, dm_local, 1)
    regrouped = lax.all_to_all(powers, "crate", split_axis=1, concat_axis=0, tiled=True)
    empty_table = jnp.zeros((SPECTRUM_BATCHES * FREQ_CHANNELS, beam_local, BINS), jnp.bfloat16)
    portion = lax.all_gather(regrouped, "board", axis=0, tiled=True)
    row_count = portion.shape[0]
    row_ids = jnp.arange(row_count, dtype=jnp.int32)
    source_board = row_ids // (crate_list * channel_groups)
    source_crate = row_ids // channel_groups % crate_list
    whole_ids = (
        source_crate * board_list + source_board
    ) * channel_groups + row_ids % channel_groups
    table = empty_table.at[whole_ids].set(portion)
    series = (
        table.reshape(FREQ_CHANNELS, SPECTRUM_BATCHES, beam_local, BINS)
        .transpose(2, 0, 1, 3)
        .reshape(beam_local, FREQ_CHANNELS, TB)
        .astype(jnp.float32)
    )
    result = dedisperse(series, dm_delays)
    return result


def solution(mesh):
    in_specs = (P(("crate", "board"), None), P(), P(), P(), P(None, "crate", None), P())
    out_specs = P("crate", "board", None)
    return jax.shard_map(shards, mesh=mesh, in_specs=in_specs, out_specs=out_specs, check_vma=False)
```

profile of v0, /device:TPU:1, one launch (start us, length us, event | category | flops | bytes accessed | tf_op | source)
XLA Modules:
  0.0 482.1 jit_solution(1558080321978159391)
XLA Ops:
  0.1 1.5 reshape.310
  1.6 2.3 multiply_convert_fusion.5
  7.0 13.7 %all-to-all-start = ((bf16[32,16,1,4,128]{4,1,3,2,0:T(8,128)(2,1)}), bf16[32,16,1,4,128]{4,1,3,2,0:T(8,128)(2,1)S(1)}, u32[]{:S(2)}, u32[]{:S(2)}) async-start(bf16[32,16,1,4,128]{4,1,3,2,0:T(8,128)(2,1)} %copy.49), calls=%async_computation | async-start | bytes 1048576 | tf_op jit(solution)/shard_map/all_to_all | solution.py:109
  21.2 11.8 %gather_fusion = s32[2048]{0:T(1024)S(1)} fusion(s32[2048]{0:T(1024)S(1)} %copy-done.1, s32[2048]{0:T(1024)S(1)} %broadcast_clamp_fusion.2), kind=kCustom, calls=%fused_computation.2 | custom fusion | bytes 24576 | tf_op jit(solution)/shard_map/jit(_take)/gather | solution.py:117
  34.1 11.8 %gather_fusion.3 = f32[2048]{0:T(1024)S(1)} fusion(f32[2048]{0:T(1024)S(1)} %bitcast.105, s32[2048]{0:T(1024)S(1)} %broadcast_clamp_fusion), kind=kCustom, calls=%fused_computation.1.clone | custom fusion | bytes 24576 | tf_op jit(solution)/shard_map/jit(_take)/gather | solution.py:119
  45.9 11.8 %gather_fusion.2 = f32[2048]{0:T(1024)S(1)} fusion(f32[2048]{0:T(1024)S(1)} %bitcast.104, s32[2048]{0:T(1024)S(1)} %broadcast_clamp_fusion), kind=kCustom, calls=%fused_computation.clone | custom fusion | bytes 24576 | tf_op jit(solution)/shard_map/jit(_take)/gather | solution.py:118
  57.7 14.5 %gather_fusion.1 = f32[2048,2,8]{2,1,0:T(2,128)} fusion(f32[2,8,2048]{1,0,2:T(2,128)S(1)} %copy.46, s32[2048]{0:T(1024)S(1)} %broadcast_clamp_fusion.1), kind=kCustom, calls=%fused_computation.3 | custom fusion | bytes 270336 | tf_op jit(solution)/shard_map/jit(_take)/gather | solution.py:120
  72.2 10.0 %select_bitcast_fusion = f32[2,8,2048]{1,0,2:T(2,128)S(1)} fusion(f32[2048,2,8]{2,1,0:T(2,128)} %gather_fusion.1, pred[2048]{0:T(1024)(128)(4,1)S(1)} %get-tuple-element.303), kind=kLoop, calls=%fused_computation.56 | loop fusion | flops 32768 | bytes 264192 | tf_op jit(solution)/shard_map/jit(_take)/select_n | solution.py:120
  83.1 8.6 %all-to-all-start.1 = ((bf16[1,16,1,128,128]{4,3,2,0,1:T(8,128)(2,1)}), bf16[1,16,1,128,128]{4,3,2,0,1:T(8,128)(2,1)}, u32[]{:S(2)}, u32[]{:S(2)}) async-start(bf16[1,16,1,128,128]{4,3,2,0,1:T(8,128)(2,1)} %copy.50), calls=%async_computation.1 | async-start | bytes 1048576 | tf_op jit(solution)/shard_map/all_to_all | solution.py:108
  91.8 1.7 fusion.92
  93.5 57.0 %dynamic-slice_reduce_fusion = (f32[2048]{0:T(1024)S(1)}, f32[2048]{0:T(1024)S(1)}) fusion(f32[1,8,2048]{1,0,2:T(1,128)S(1)} %get-tuple-element.308, s32[]{:T(128)S(6)} %select_n.164, f32[1,8,2048]{1,0,2:T(1,128)S(1)} %get-tuple-element.309), kind=kLoop, calls=%fused_computation.65 | loop fusion | bytes 32772 | tf_op jit(solution)/shard_map/while/body/eval_jaxpr/jit(dynamic_index_in_dim)/dynamic_slice | solution.py:133
  150.6 48.7 %while.33 = (s32[]{:T(128)}, bf16[2,256,16]{1,2,0:T(8,128)(2,1)S(1)}, f32[2048]{0:T(1024)S(1)}, f32[]{:T(128)}, f32[2,2,256]{2,1,0:T(2,128)S(1)}, /*index=5*/f32...) while((s32[]{:T(128)}, ...), condition=%wide.region_2.4_spmd, body=%wide.region_0.3_spmd.sunk | while | flops 277975040 | bytes 1949857 | solution.py:148
  162.4 9.1 %fusion.116 = f32[256,128]{0,1:T(8,128)S(1)} fusion(bf16[2048,128]{1,0:T(8,128)(2,1)} %get-tuple-element.456, f32[2048]{0:T(1024)S(1)} %get-tuple-element.455, f32[2048]{0:T(1024)S(1)} %get-tuple-element.454, f32[256]{0:T(256)S(1)} %bitcast.120, f32[2048]{0:T(1024)S(1)} %get-tuple-element.453, f32[256]{0:T(256)S(1)} %bitcast.118, ...), kind=kOutput, calls=%fused_computation.10.clone.1 | convolution fusion | flops 138936320 | bytes 690180 | tf_op jit(solution)/shard_map/while/body/eval_jaxpr/while/body/eval_jaxpr/dot_general | solution.py:139
  171.5 9.1 %fusion.115 = f32[256,128]{0,1:T(8,128)S(1)} fusion(bf16[2048,128]{1,0:T(8,128)(2,1)} %get-tuple-element.456, f32[2048]{0:T(1024)S(1)} %get-tuple-element.455, f32[2048]{0:T(1024)S(1)} %get-tuple-element.454, f32[256]{0:T(256)S(1)} %bitcast.121, f32[2048]{0:T(1024)S(1)} %get-tuple-element.453, f32[256]{0:T(256)S(1)} %bitcast.119, ...), kind=kOutput, calls=%fused_computation.11.clone.1 | convolution fusion | flops 138936320 | bytes 690180 | tf_op jit(solution)/shard_map/while/body/eval_jaxpr/while/body/eval_jaxpr/dot_general | solution.py:140
  180.8 9.1 %fusion.116 = f32[256,128]{0,1:T(8,128)S(1)} fusion(bf16[2048,128]{1,0:T(8,128)(2,1)} %get-tuple-element.456, f32[2048]{0:T(1024)S(1)} %get-tuple-element.455, f32[2048]{0:T(1024)S(1)} %get-tuple-element.454, f32[256]{0:T(256)S(1)} %bitcast.120, f32[2048]{0:T(1024)S(1)} %get-tuple-element.453, f32[256]{0:T(256)S(1)} %bitcast.118, ...), kind=kOutput, calls=%fused_computation.10.clone.1 | convolution fusion | flops 138936320 | bytes 690180 | tf_op jit(solution)/shard_map/while/body/eval_jaxpr/while/body/eval_jaxpr/dot_general | solution.py:139
  189.9 9.1 %fusion.115 = f32[256,128]{0,1:T(8,128)S(1)} fusion(bf16[2048,128]{1,0:T(8,128)(2,1)} %get-tuple-element.456, f32[2048]{0:T(1024)S(1)} %get-tuple-element.455, f32[2048]{0:T(1024)S(1)} %get-tuple-element.454, f32[256]{0:T(256)S(1)} %bitcast.121, f32[2048]{0:T(1024)S(1)} %get-tuple-element.453, f32[256]{0:T(256)S(1)} %bitcast.119, ...), kind=kOutput, calls=%fused_computation.11.clone.1 | convolution fusion | flops 138936320 | bytes 690180 | tf_op jit(solution)/shard_map/while/body/eval_jaxpr/while/body/eval_jaxpr/dot_general | solution.py:140
  200.0 1.4 reduce.4
  202.2 9.5 %all-to-all-start.2 = ((bf16[32,2,128]{2,1,0:T(2,128)(2,1)}), bf16[32,2,128]{2,1,0:T(2,128)(2,1)S(1)}, u32[]{:S(2)}, u32[]{:S(2)}) async-start(bf16[32,2,128]{2,1,0:T(2,128)(2,1)} %reshape.373), calls=%async_computation.2 | async-start | bytes 32768 | tf_op jit(solution)/shard_map/all_to_all | solution.py:154
  211.8 8.5 %all-to-all-done.2 = bf16[32,2,128]{2,1,0:T(2,128)(2,1)S(1)} async-done(((bf16[32,2,128]{2,1,0:T(2,128)(2,1)}), bf16[32,2,128]{2,1,0:T(2,128)(2,1)S(1)}, u32[]{:S(2)}, u32[]{:S(2)}) %all-to-all-start.2) | async-done | bytes 16416 | tf_op jit(solution)/shard_map/all_to_all | solution.py:154
  220.7 24.8 %all_gather.3 = bf16[512,16,16]{1,0,2:T(8,128)(2,1)S(1)} all-gather(bf16[32,16,16]{1,0,2:T(8,128)(2,1)S(1)} %all_to_all.35), channel_id=1, replica_groups=mesh['crate'=32,'board'=16] {'board'}, dimensions={0}, use_global_device_ids=true | all-gather | bytes 278528 | tf_op jit(solution)/shard_map/all_gather | solution.py:156
  245.5 3.1 copy.54
  248.9 33.1 %scatter_fusion = bf16[512,16,16]{2,1,0:T(8,128)(2,1)S(1)} fusion(bf16[512,16,16]{2,1,0:T(8,128)(2,1)S(1)} %broadcast_in_dim.62, s32[512]{0:T(512)S(1)} %bitcast.123, bf16[512,16,16]{2,1,0:T(8,128)(2,1)} %copy.54), kind=kCustom, calls=%fused_computation.4 | custom fusion | bytes 788480 | tf_op jit(solution)/shard_map/scatter | solution.py:164
  282.0 1.9 copy.55
  284.8 195.4 %while.34 = (s32[]{:T(128)}, f32[32,32,16]{1,0,2:T(8,128)S(1)}, f32[32,32,16]{1,0,2:T(8,128)S(1)}, s32[32]{0:T(128)S(1)}, s32[256,32]{1,0:T(8,128)S(1)}, /*index...) while((s32[]{:T(128)}, f32[32,32,16]{1,0,2:T(8,128)S(1)}, ...), condition=%wide.region_5.7_spmd, body=%wide.region_4.6_spmd.sunk | while | flops 6751234 | bytes 282757 | solution.py:73
  286.8 1.3 convolution_add_fusion.2
  289.5 1.3 convolution_subtract_fusion.3
  292.9 1.3 convolution_add_fusion.2
  295.6 1.3 convolution_subtract_fusion.3
  299.0 1.3 convolution_add_fusion.2
  301.7 1.3 convolution_subtract_fusion.3
  305.1 1.3 convolution_add_fusion.2
  307.8 1.3 convolution_subtract_fusion.3
  (312 shorter events, 193.0 us)
Async XLA Ops:
  0.0 91.7 %copy-start = (s32[256,512]{1,0:T(8,128)S(1)}, s32[256,512]{1,0:T(8,128)}, u32[]{:S(2)}) copy-start(s32[256,512]{1,0:T(8,128)} %param.17) | copy-start | bytes 1572868
  5.6 15.5 %copy-start.4 = (f32[2,2048]{1,0:T(2,128)S(1)}, f32[2,2048]{1,0:T(2,128)}, u32[]{:S(2)}) copy-start(f32[2,2048]{1,0:T(2,128)} %param.14) | copy-start | bytes 49156
  5.6 15.6 %copy-start.1 = (s32[2048]{0:T(1024)S(1)}, s32[2048]{0:T(1024)}, u32[]{:S(2)}) copy-start(s32[2048]{0:T(1024)} %param.13) | copy-start | bytes 24580
  7.0 75.2 %all-to-all-start = ((bf16[32,16,1,4,128]{4,1,3,2,0:T(8,128)(2,1)}), bf16[32,16,1,4,128]{4,1,3,2,0:T(8,128)(2,1)S(1)}, u32[]{:S(2)}, u32[]{:S(2)}) async-start(bf16[32,16,1,4,128]{4,1,3,2,0:T(8,128)(2,1)} %copy.49), calls=%async_computation | async-start | bytes 1048576 | tf_op jit(solution)/shard_map/all_to_all | solution.py:109
  21.2 11.8 %copy-start.2 = (f32[2,8,2048]{2,1,0:T(8,128)S(1)}, f32[2,8,2048]{2,1,0:T(8,128)}, u32[]{:S(2)}) copy-start(f32[2,8,2048]{2,1,0:T(8,128)} %param.16) | copy-start | bytes 393220
  83.1 67.5 %all-to-all-start.1 = ((bf16[1,16,1,128,128]{4,3,2,0,1:T(8,128)(2,1)}), bf16[1,16,1,128,128]{4,3,2,0,1:T(8,128)(2,1)}, u32[]{:S(2)}, u32[]{:S(2)}) async-start(bf16[1,16,1,128,128]{4,3,2,0,1:T(8,128)(2,1)} %copy.50), calls=%async_computation.1 | async-start | bytes 1048576 | tf_op jit(solution)/shard_map/all_to_all | solution.py:108
  93.5 57.1 %copy-start.3 = (f32[2,512]{1,0:T(2,128)S(1)}, f32[2,512]{1,0:T(2,128)}, u32[]{:S(2)}) copy-start(f32[2,512]{1,0:T(2,128)} %param.15) | copy-start | bytes 12292
  202.2 18.0 %all-to-all-start.2 = ((bf16[32,2,128]{2,1,0:T(2,128)(2,1)}), bf16[32,2,128]{2,1,0:T(2,128)(2,1)S(1)}, u32[]{:S(2)}, u32[]{:S(2)}) async-start(bf16[32,2,128]{2,1,0:T(2,128)(2,1)} %reshape.373), calls=%async_computation.2 | async-start | bytes 32768 | tf_op jit(solution)/shard_map/all_to_all | solution.py:154
where the time goes:
time: 490 us; the launch traced here: 482 us
  matrix products  208 us (42%)
  local copies, waits for them, and re-layouts  180 us (37%)
  starting transfers between devices  31.8 us (6%)
  blocking collectives  24.8 us (5%)
  loops' own time  14.4 us (3%)
  other arithmetic  14.1 us (3%)
  waiting for transfers between devices  8.51 us (2%)
    dynamic_slice x1, local copies, waits for them, and re-layouts, group_power(): lax.dynamic_index_in_dim(gains_slot[1], gain_row, 0, keepdims=False)  57 us
    dot_general x32, matrix products, per_freq(): jnp.einsum('cd,cb->db', shift_im, part_re, precision=lax.Precision.HIGHEST)  42.6 us
    dot_general x32, matrix products, per_freq(): jnp.einsum('cd,cb->db', shift_im, part_im, precision=lax.Precision.HIGHEST)  42.6 us
    dot_general x32, matrix products, per_freq(): jnp.einsum('cd,cb->db', shift_re, part_re, precision=lax.Precision.HIGHEST)  42.1 us
    dot_general x32, matrix products, per_freq(): jnp.einsum('cd,cb->db', shift_re, part_im, precision=lax.Precision.HIGHEST)  42 us
    scatter x1, local copies, waits for them, and re-layouts, shards(): table = empty_table.at[whole_ids].set(portion)  33.1 us
    all_gather x1, blocking collectives, shards(): portion = lax.all_gather(regrouped, 'board', axis=0, tiled=True)  24.8 us
    dynamic_slice x64, local copies, waits for them, and re-layouts, dedisperse(): freq_re, freq_im = lax.map(per_freq, (bin_ids, spec_re, spec_im))  20 us
  transfers between devices with their start and end apart: 3, of which 1 were waited for; matrix products, arithmetic and copies ran while one was open for 25% of the time, Pallas kernels for 0%

commit v1 on v0

--- a/solution.py
+++ b/solution.py
@@ -3,6 +3,7 @@
 import jax.numpy as jnp
 from jax import lax
 from jax.sharding import PartitionSpec as P
+from jax.lax import all_to_all, axis_size
 
 ANTENNA_INPUTS = 2048
 FREQ_CHANNELS = 256
@@ -153,7 +154,10 @@
     dm_delays = lax.dynamic_slice_in_dim(delays, board_index * dm_local, dm_local, 1)
     regrouped = lax.all_to_all(powers, "crate", split_axis=1, concat_axis=0, tiled=True)
     empty_table = jnp.zeros((SPECTRUM_BATCHES * FREQ_CHANNELS, beam_local, BINS), jnp.bfloat16)
-    portion = lax.all_gather(regrouped, "board", axis=0, tiled=True)
+    top = all_to_all(
+        jnp.stack(tuple((regrouped for _ in range(axis_size("board"))))), "board", 0, 0
+    )
+    portion = jnp.concatenate(top, axis=0)
     row_count = portion.shape[0]
     row_ids = jnp.arange(row_count, dtype=jnp.int32)
     source_board = row_ids // (crate_list * channel_groups)

time: 490 us -> 473 us (0.965)
  loops' own time: 14.4 us -> 2.84 us
  blocking collectives: 24.8 us -> 17.9 us
    all_gather x1 -> x0, blocking collectives: 24.8 us -> none  [shards(): portion = lax.all_gather(regrouped, 'board', axis=0, tiled=True)]
    all_to_all x0 -> x1, blocking collectives: none -> 17.9 us  [shards(): lax.all_to_all(powers, 'crate', split_axis=1, concat_axis=0, tiled=True)]
    another operation x1, loops' own time: 12.1 us -> 0.52 us  [group_power(): return lax.map(block_power, dir_blocks).reshape(BEAMS, BINS)]
where the time goes in v1:
time: 473 us; the launch traced here: 464 us
  matrix products  208 us (44%)
  local copies, waits for them, and re-layouts  181 us (38%)
  starting transfers between devices  30.6 us (6%)
  blocking collectives  17.9 us (4%)
  other arithmetic  11.6 us (2%)
  waiting for transfers between devices  11.4 us (2%)
    dynamic_slice x1, local copies, waits for them, and re-layouts, group_power(): lax.dynamic_index_in_dim(gains_slot[1], gain_row, 0, keepdims=False)  57.5 us
    dot_general x32, matrix products, per_freq(): jnp.einsum('cd,cb->db', shift_im, part_re, precision=lax.Precision.HIGHEST)  42.6 us
    dot_general x32, matrix products, per_freq(): jnp.einsum('cd,cb->db', shift_im, part_im, precision=lax.Precision.HIGHEST)  42.6 us
    dot_general x32, matrix products, per_freq(): jnp.einsum('cd,cb->db', shift_re, part_re, precision=lax.Precision.HIGHEST)  42.1 us
    dot_general x32, matrix products, per_freq(): jnp.einsum('cd,cb->db', shift_re, part_im, precision=lax.Precision.HIGHEST)  42 us
    scatter x1, local copies, waits for them, and re-layouts, shards(): table = empty_table.at[whole_ids].set(portion)  33.1 us
    dynamic_slice x64, local copies, waits for them, and re-layouts, dedisperse(): freq_re, freq_im = lax.map(per_freq, (bin_ids, spec_re, spec_im))  20 us
    dot_general x2, matrix products, block_power(): imag_side = jnp.dot(weight_im, columns, preferred_element_type=jnp.float32)  18.2 us
  transfers between devices with their start and end apart: 3, of which 1 were waited for; matrix products, arithmetic and copies ran while one was open for 25% of the time, Pallas kernels for 0%

profile of v1, /device:TPU:1, one launch (start us, length us, event | category | flops | bytes accessed | tf_op | source)
XLA Modules:
  0.0 464.4 jit_solution(4997370888509128410)
XLA Ops:
  0.1 1.5 reshape.315
  1.6 2.3 multiply_convert_fusion.5
  7.0 13.8 %all-to-all-start = ((bf16[32,16,1,4,128]{4,1,3,2,0:T(8,128)(2,1)}), bf16[32,16,1,4,128]{4,1,3,2,0:T(8,128)(2,1)S(1)}, u32[]{:S(2)}, u32[]{:S(2)}) async-start(bf16[32,16,1,4,128]{4,1,3,2,0:T(8,128)(2,1)} %copy.81), calls=%async_computation | async-start | bytes 1048576 | tf_op jit(solution)/shard_map/all_to_all | solution.py:110
  22.3 11.8 %gather_fusion = s32[2048]{0:T(1024)S(1)} fusion(s32[2048]{0:T(1024)S(1)} %copy-done.1, s32[2048]{0:T(1024)S(1)} %broadcast_clamp_fusion.2), kind=kCustom, calls=%fused_computation.2 | custom fusion | bytes 24576 | tf_op jit(solution)/shard_map/jit(_take)/gather | solution.py:118
  34.1 11.8 %gather_fusion.3 = f32[2048]{0:T(1024)S(1)} fusion(f32[2048]{0:T(1024)S(1)} %bitcast.108, s32[2048]{0:T(1024)S(1)} %broadcast_clamp_fusion), kind=kCustom, calls=%fused_computation.1.clone | custom fusion | bytes 24576 | tf_op jit(solution)/shard_map/jit(_take)/gather | solution.py:120
  45.9 11.8 %gather_fusion.2 = f32[2048]{0:T(1024)S(1)} fusion(f32[2048]{0:T(1024)S(1)} %bitcast.107, s32[2048]{0:T(1024)S(1)} %broadcast_clamp_fusion), kind=kCustom, calls=%fused_computation.clone | custom fusion | bytes 24576 | tf_op jit(solution)/shard_map/jit(_take)/gather | solution.py:119
  57.8 14.5 %gather_fusion.1 = f32[2048,2,8]{2,1,0:T(2,128)} fusion(f32[2,8,2048]{1,0,2:T(2,128)S(1)} %copy.78, s32[2048]{0:T(1024)S(1)} %broadcast_clamp_fusion.1), kind=kCustom, calls=%fused_computation.3 | custom fusion | bytes 270336 | tf_op jit(solution)/shard_map/jit(_take)/gather | solution.py:121
  73.2 8.1 %all-to-all-start.1 = ((bf16[1,16,1,128,128]{4,3,2,0,1:T(8,128)(2,1)}), bf16[1,16,1,128,128]{4,3,2,0,1:T(8,128)(2,1)}, u32[]{:S(2)}, u32[]{:S(2)}) async-start(bf16[1,16,1,128,128]{4,3,2,0,1:T(8,128)(2,1)} %copy.82), calls=%async_computation.1 | async-start | bytes 1048576 | tf_op jit(solution)/shard_map/all_to_all | solution.py:109
  81.3 7.4 %select_bitcast_fusion = f32[2,8,2048]{1,0,2:T(2,128)S(1)} fusion(f32[2048,2,8]{2,1,0:T(2,128)S(1)} %copy-done.2, pred[2048]{0:T(1024)(128)(4,1)S(1)} %get-tuple-element.317), kind=kLoop, calls=%fused_computation.56 | loop fusion | flops 32768 | bytes 264192 | tf_op jit(solution)/shard_map/jit(_take)/select_n | solution.py:121
  88.7 1.7 fusion.92
  90.4 57.5 %dynamic-slice_reduce_fusion = (f32[2048]{0:T(1024)S(1)}, f32[2048]{0:T(1024)S(1)}) fusion(f32[1,8,2048]{1,0,2:T(1,128)S(1)} %get-tuple-element.322, s32[]{:T(128)S(6)} %select_n.164, f32[1,8,2048]{1,0,2:T(1,128)S(1)} %get-tuple-element.323), kind=kLoop, calls=%fused_computation.65 | loop fusion | bytes 32772 | tf_op jit(solution)/shard_map/while/body/eval_jaxpr/jit(dynamic_index_in_dim)/dynamic_slice | solution.py:134
  147.9 37.1 %while.33 = (s32[]{:T(128)}, bf16[2,256,16]{1,2,0:T(8,128)(2,1)S(1)}, f32[2048]{0:T(1024)S(1)}, f32[]{:T(128)}, f32[2,2,256]{2,1,0:T(2,128)S(1)}, /*index=5*/f32...) while((s32[]{:T(128)}, ...), condition=%wide.region_2.4_spmd, body=%wide.region_0.3_spmd.sunk | while | flops 277975040 | bytes 1949857 | solution.py:149
  148.1 9.1 %fusion.116 = f32[256,128]{0,1:T(8,128)S(1)} fusion(bf16[2048,128]{1,0:T(8,128)(2,1)} %get-tuple-element.470, f32[2048]{0:T(1024)S(1)} %get-tuple-element.469, f32[2048]{0:T(1024)S(1)} %get-tuple-element.468, f32[256]{0:T(256)S(1)} %bitcast.126, f32[2048]{0:T(1024)S(1)} %get-tuple-element.467, f32[256]{0:T(256)S(1)} %bitcast.124, ...), kind=kOutput, calls=%fused_computation.10.clone.1 | convolution fusion | flops 138936320 | bytes 690180 | tf_op jit(solution)/shard_map/while/body/eval_jaxpr/while/body/eval_jaxpr/dot_general | solution.py:140
  157.3 9.1 %fusion.115 = f32[256,128]{0,1:T(8,128)S(1)} fusion(bf16[2048,128]{1,0:T(8,128)(2,1)} %get-tuple-element.470, f32[2048]{0:T(1024)S(1)} %get-tuple-element.469, f32[2048]{0:T(1024)S(1)} %get-tuple-element.468, f32[256]{0:T(256)S(1)} %bitcast.127, f32[2048]{0:T(1024)S(1)} %get-tuple-element.467, f32[256]{0:T(256)S(1)} %bitcast.125, ...), kind=kOutput, calls=%fused_computation.11.clone.1 | convolution fusion | flops 138936320 | bytes 690180 | tf_op jit(solution)/shard_map/while/body/eval_jaxpr/while/body/eval_jaxpr/dot_general | solution.py:141
  166.5 9.1 %fusion.116 = f32[256,128]{0,1:T(8,128)S(1)} fusion(bf16[2048,128]{1,0:T(8,128)(2,1)} %get-tuple-element.470, f32[2048]{0:T(1024)S(1)} %get-tuple-element.469, f32[2048]{0:T(1024)S(1)} %get-tuple-element.468, f32[256]{0:T(256)S(1)} %bitcast.126, f32[2048]{0:T(1024)S(1)} %get-tuple-element.467, f32[256]{0:T(256)S(1)} %bitcast.124, ...), kind=kOutput, calls=%fused_computation.10.clone.1 | convolution fusion | flops 138936320 | bytes 690180 | tf_op jit(solution)/shard_map/while/body/eval_jaxpr/while/body/eval_jaxpr/dot_general | solution.py:140
  175.6 9.1 %fusion.115 = f32[256,128]{0,1:T(8,128)S(1)} fusion(bf16[2048,128]{1,0:T(8,128)(2,1)} %get-tuple-element.470, f32[2048]{0:T(1024)S(1)} %get-tuple-element.469, f32[2048]{0:T(1024)S(1)} %get-tuple-element.468, f32[256]{0:T(256)S(1)} %bitcast.127, f32[2048]{0:T(1024)S(1)} %get-tuple-element.467, f32[256]{0:T(256)S(1)} %bitcast.125, ...), kind=kOutput, calls=%fused_computation.11.clone.1 | convolution fusion | flops 138936320 | bytes 690180 | tf_op jit(solution)/shard_map/while/body/eval_jaxpr/while/body/eval_jaxpr/dot_general | solution.py:141
  185.8 1.4 reduce.4
  187.4 17.9 %all_to_all.41 = bf16[32,2,128]{2,1,0:T(2,128)(2,1)S(1)} all-to-all(bf16[32,2,128]{2,1,0:T(2,128)(2,1)S(1)} %reshape.380), channel_id=1, replica_groups=mesh['crate'=32,'board'=16] {'crate'}, dimensions={0} | all-to-all | bytes 32768 | tf_op jit(solution)/shard_map/all_to_all | solution.py:155
  205.9 1.7 reshape.382
  207.6 8.7 %all-to-all-start.3 = ((bf16[16,2,4096]{2,1,0:T(2,128)(2,1)}), bf16[16,2,4096]{2,1,0:T(2,128)(2,1)S(1)}, u32[]{:S(2)}, u32[]{:S(2)}) async-start(bf16[16,2,4096]{2,1,0:T(2,128)(2,1)} %reshape.382), calls=%async_computation.3 | async-start | bytes 524288 | tf_op jit(solution)/shard_map/all_to_all | solution.py:157
  216.4 11.4 %all-to-all-done.3 = bf16[16,2,4096]{2,1,0:T(2,128)(2,1)S(1)} async-done(((bf16[16,2,4096]{2,1,0:T(2,128)(2,1)}), bf16[16,2,4096]{2,1,0:T(2,128)(2,1)S(1)}, u32[]{:S(2)}, u32[]{:S(2)}) %all-to-all-start.3) | async-done | bytes 262176 | tf_op jit(solution)/shard_map/all_to_all | solution.py:157
  228.4 2.6 copy.97
  231.2 33.1 %scatter_fusion = bf16[512,16,16]{2,1,0:T(8,128)(2,1)S(1)} fusion(bf16[512,16,16]{2,1,0:T(8,128)(2,1)S(1)} %broadcast_in_dim.62, s32[512]{0:T(512)S(1)} %bitcast.129, bf16[512,16,16]{2,1,0:T(8,128)(2,1)} %bitcast.110), kind=kCustom, calls=%fused_computation.4 | custom fusion | bytes 788480 | tf_op jit(solution)/shard_map/scatter | solution.py:168
  264.3 1.9 copy.89
  267.1 195.4 %while.34 = (s32[]{:T(128)}, f32[32,32,16]{1,0,2:T(8,128)S(1)}, f32[32,32,16]{1,0,2:T(8,128)S(1)}, s32[32]{0:T(128)S(1)}, s32[256,32]{1,0:T(8,128)S(1)}, /*index...) while((s32[]{:T(128)}, f32[32,32,16]{1,0,2:T(8,128)S(1)}, ...), condition=%wide.region_5.7_spmd, body=%wide.region_4.6_spmd.sunk | while | flops 6751234 | bytes 282757 | solution.py:74
  269.1 1.3 convolution_add_fusion.2
  271.8 1.3 convolution_subtract_fusion.3
  275.2 1.3 convolution_add_fusion.2
  277.9 1.3 convolution_subtract_fusion.3
  281.3 1.3 convolution_add_fusion.2
  284.0 1.3 convolution_subtract_fusion.3
  287.4 1.3 convolution_add_fusion.2
  (317 shorter events, 194.3 us)
Async XLA Ops:
  0.0 216.3 %copy-start = (s32[256,512]{1,0:T(8,128)S(1)}, s32[256,512]{1,0:T(8,128)}, u32[]{:S(2)}) copy-start(s32[256,512]{1,0:T(8,128)} %param.17) | copy-start | bytes 1572868
  5.6 15.7 %copy-start.5 = (f32[2,2048]{1,0:T(2,128)S(1)}, f32[2,2048]{1,0:T(2,128)}, u32[]{:S(2)}) copy-start(f32[2,2048]{1,0:T(2,128)} %param.14) | copy-start | bytes 49156
  5.6 15.7 %copy-start.3 = (f32[2,8,2048]{2,1,0:T(8,128)S(1)}, f32[2,8,2048]{2,1,0:T(8,128)}, u32[]{:S(2)}) copy-start(f32[2,8,2048]{2,1,0:T(8,128)} %param.16) | copy-start | bytes 393220
  7.0 15.3 %copy-start.1 = (s32[2048]{0:T(1024)S(1)}, s32[2048]{0:T(1024)}, u32[]{:S(2)}) copy-start(s32[2048]{0:T(1024)} %param.13) | copy-start | bytes 24580
  7.0 65.3 %all-to-all-start = ((bf16[32,16,1,4,128]{4,1,3,2,0:T(8,128)(2,1)}), bf16[32,16,1,4,128]{4,1,3,2,0:T(8,128)(2,1)S(1)}, u32[]{:S(2)}, u32[]{:S(2)}) async-start(bf16[32,16,1,4,128]{4,1,3,2,0:T(8,128)(2,1)} %copy.81), calls=%async_computation | async-start | bytes 1048576 | tf_op jit(solution)/shard_map/all_to_all | solution.py:110
  72.2 9.0 %copy-start.2 = (f32[2048,2,8]{2,1,0:T(2,128)S(1)}, f32[2048,2,8]{2,1,0:T(2,128)}, u32[]{:S(2)}) copy-start(f32[2048,2,8]{2,1,0:T(2,128)} %gather_fusion.1) | copy-start | bytes 393220
  73.2 74.7 %all-to-all-start.1 = ((bf16[1,16,1,128,128]{4,3,2,0,1:T(8,128)(2,1)}), bf16[1,16,1,128,128]{4,3,2,0,1:T(8,128)(2,1)}, u32[]{:S(2)}, u32[]{:S(2)}) async-start(bf16[1,16,1,128,128]{4,3,2,0,1:T(8,128)(2,1)} %copy.82), calls=%async_computation.1 | async-start | bytes 1048576 | tf_op jit(solution)/shard_map/all_to_all | solution.py:109
  90.4 57.5 %copy-start.4 = (f32[2,512]{1,0:T(2,128)S(1)}, f32[2,512]{1,0:T(2,128)}, u32[]{:S(2)}) copy-start(f32[2,512]{1,0:T(2,128)} %param.15) | copy-start | bytes 12292
  207.6 20.2 %all-to-all-start.3 = ((bf16[16,2,4096]{2,1,0:T(2,128)(2,1)}), bf16[16,2,4096]{2,1,0:T(2,128)(2,1)S(1)}, u32[]{:S(2)}, u32[]{:S(2)}) async-start(bf16[16,2,4096]{2,1,0:T(2,128)(2,1)} %reshape.382), calls=%async_computation.3 | async-start | bytes 524288 | tf_op jit(solution)/shard_map/all_to_all | solution.py:157
